TPU v7x, 32 devices: a whole 2x2x4 slice. The times are simulated.
32 devices in a mesh: bucket: 16 (over z, y, core), edge: 2 (over x).
Axes of the slice: x: 2, y: 2, z: 4, core: 2. Of those that a mesh axis runs over, the one named last changes fastest.
Arguments:
- left_slab: bfloat16 [6144, 256], P(('bucket', 'edge')), may hold values from -1.5 to 1.5
- right_slab: bfloat16 [6144, 256], P(('bucket', 'edge')), may hold values from -1.5 to 1.5
- relation: float32 [1024, 256], replicated, may hold values from 0.5 to 1.5
- src_ids: int32 [2, 16, 4096], P(None, 'bucket', 'edge'), may hold values from 0 to 383
- dst_ids: int32 [2, 16, 4096], P(None, 'bucket', 'edge'), may hold values from 0 to 383
- rel_ids: int32 [2, 16, 4096], P(None, 'bucket', 'edge'), may hold values from 0 to 1023
- neg_ids: int32 [2, 16, 16, 512], P(None, 'bucket', 'edge'), may hold values from 0 to 383
- edge_counts: int32 [2, 16], P(None, 'bucket'), may hold values from 1 to 4096, as said below
Outputs:
- left_out: bfloat16 [6144, 256], P(('bucket', 'edge'))
- right_out: bfloat16 [6144, 256], P(('bucket', 'edge'))
- relation_out: float32 [1024, 256], replicated
Inputs may be any that keep to these rules, and one draw needn't show every extreme that they name: `edge_counts`: live edges are the first slots of a bucket; in every round some bucket has all 4096 slots live.
All inputs are finite; a program needn't handle non-finite values.
Results may differ from a plain program's by a relative error of at most 0.0046.
Values may be sent and summed in bfloat16 or wider, within the bound.
A program may use at most 64 MiB of HBM per device.

v0:
```python
import jax
import jax.numpy as jnp
from jax import lax
from jax.sharding import PartitionSpec as P

ROUNDS = 2
learn_rate = 0.05
relation_rate = 0.05


def from_behind(block, axis, distance):
    devices = range(lax.axis_size(axis))
    route = [((i - distance) % len(devices), i) for i in devices]
    return lax.ppermute(block, axis, route)


def span_grads(left, right, theta, src_c, dst_c, rel_c, neg_c, mask):
    s_rows = left[src_c]
    d_rows = right[dst_c]
    negatives = right[neg_c]
    t_rows = theta[rel_c]
    s_wide = s_rows.astype(jnp.float32)
    q_rows = (s_wide * t_rows).astype(jnp.bfloat16)
    q_wide = q_rows.astype(jnp.float32)
    d_wide = d_rows.astype(jnp.float32)
    pos = jnp.sum(q_wide * d_wide, axis=-1)
    scores = jnp.dot(q_rows, negatives.T, preferred_element_type=jnp.float32)
    g_pos = -jax.nn.sigmoid(-pos) * mask
    g_neg = (jax.nn.sigmoid(scores) * mask[:, None]).astype(jnp.bfloat16)
    g_q = g_pos[:, None] * d_wide + jnp.dot(g_neg, negatives, preferred_element_type=jnp.float32)
    g_d = g_pos[:, None] * q_wide
    g_negrows = jnp.dot(g_neg.T, q_rows, preferred_element_type=jnp.float32)
    g_s = g_q * t_rows
    g_t = g_q * s_wide
    return (g_s, g_d, g_negrows, g_t)


def train(full_left, full_right, theta, src, dst, rel, neg, block_ids, count):
    width = src.shape[1]
    n_live = jnp.sum((block_ids * width < count).astype(jnp.int32))

    def step(c, carry):
        g_left, g_right, g_theta = carry
        src_c = lax.dynamic_index_in_dim(src, c, 0, keepdims=False)
        dst_c = lax.dynamic_index_in_dim(dst, c, 0, keepdims=False)
        rel_c = lax.dynamic_index_in_dim(rel, c, 0, keepdims=False)
        neg_c = lax.dynamic_index_in_dim(neg, c, 0, keepdims=False)
        first = lax.dynamic_index_in_dim(block_ids, c, 0, keepdims=False) * width
        mask = (first + jnp.arange(width) < count).astype(jnp.float32)
        g_s, g_d, g_negrows, g_t = span_grads(
            full_left, full_right, theta, src_c, dst_c, rel_c, neg_c, mask
        )
        g_left = g_left.at[src_c].add(g_s)
        g_right = g_right.at[dst_c].add(g_d).at[neg_c].add(g_negrows)
        g_theta = g_theta.at[rel_c].add(g_t)
        return (g_left, g_right, g_theta)

    rows = full_left.shape[0]
    init = (
        jnp.zeros((rows, full_left.shape[1]), jnp.float32),
        jnp.zeros((rows, full_left.shape[1]), jnp.float32),
        jnp.zeros(theta.shape, jnp.float32),
    )
    return lax.fori_loop(0, n_live, step, init)


def relation_sum(g_theta):
    return lax.psum(g_theta, ("bucket", "edge"))


def descend(slab, grad):
    return (slab.astype(jnp.float32) - learn_rate * grad).astype(jnp.bfloat16)


def body(left_slab, right_slab, relation, src_ids, dst_ids, rel_ids, neg_ids, edge_counts):
    me = lax.axis_index("edge")
    blocks = neg_ids.shape[2]
    width = src_ids.shape[2] // blocks
    negs = neg_ids.shape[3]
    src = src_ids.reshape(ROUNDS, blocks, width)
    dst = dst_ids.reshape(ROUNDS, blocks, width)
    rel = rel_ids.reshape(ROUNDS, blocks, width)
    neg = neg_ids.reshape(ROUNDS, blocks, negs)
    positions = jnp.arange(blocks, dtype=jnp.int32)
    block_ids = me * blocks + positions
    theta = relation
    left_out = left_slab
    right_out = right_slab
    for rnd in range(ROUNDS):
        if rnd > 0:
            right_out = from_behind(right_out, "bucket", 1)
        full_left, full_right = (
            lax.all_gather(left_out, "edge", axis=0, tiled=True),
            lax.all_gather(right_out, "edge", axis=0, tiled=True),
        )
        g_left, g_right, g_theta = train(
            full_left,
            full_right,
            theta,
            src[rnd],
            dst[rnd],
            rel[rnd],
            neg[rnd],
            block_ids,
            edge_counts[rnd, 0],
        )
        g_left, g_right = (
            lax.psum_scatter(g_left, "edge", scatter_dimension=0, tiled=True),
            lax.psum_scatter(g_right, "edge", scatter_dimension=0, tiled=True),
        )
        left_out = descend(left_out, g_left)
        right_out = descend(right_out, g_right)
        theta = theta - relation_rate * relation_sum(g_theta)
    return (left_out, right_out, theta)


def solution(mesh):
    placed = (
        P(("bucket", "edge"), None),
        P(("bucket", "edge"), None),
        P(),
        P(None, "bucket", "edge"),
        P(None, "bucket", "edge"),
        P(None, "bucket", "edge"),
        P(None, "bucket", "edge", None),
        P(None, "bucket"),
    )
    return jax.shard_map(
        body,
        mesh=mesh,
        in_specs=placed,
        out_specs=(P(("bucket", "edge"), None), P(("bucket", "edge"), None), P()),
        check_vma=False,
    )
```

profile of v0, /device:TPU:0, one launch (start us, length us, event | category | flops | bytes accessed | tf_op | source)
XLA Modules:
  0.0 697.3 jit_solution(16866233475655808648)
XLA Ops:
  12.7 6.5 all_gather.12
  19.3 5.4 all_gather.13
  27.8 73.1 %while.28 = (s32[]{:T(128)}, f32[384,256]{1,0:T(8,128)}, f32[384,256]{1,0:T(8,128)S(1)}, f32[1024,256]{1,0:T(8,128)}, s32[]{:T(128)}, /*index=5*/s32[8,256]{1,0:...) while((s32[]{:T(128)}, f32[384,256]{1,0:T(8,128)}, ...), condition=%wide.region_7.8_spmd, body=%wide.region_1.7_spmd.sunk | while | flops 203302656 | bytes 9221379 | solution.py:64
  34.2 2.0 gather_fusion.3
  38.4 3.6 scatter_custom_fusion.31
  42.3 2.2 scatter_custom_fusion.32
  44.5 3.5 scatter_fusion
  48.0 4.0 scatter_custom_fusion.34
  58.4 2.0 gather_fusion.3
  62.6 3.6 scatter_custom_fusion.31
  66.4 2.2 scatter_custom_fusion.32
  68.6 3.5 scatter_fusion
  72.1 4.0 scatter_custom_fusion.34
  82.5 2.0 gather_fusion.3
  86.7 3.6 scatter_custom_fusion.31
  90.5 2.2 scatter_custom_fusion.32
  92.8 3.5 scatter_fusion
  96.3 4.0 scatter_custom_fusion.34
  104.3 250.2 %all-reduce.3.cloned.1.call-done = f32[1024,256]{1,0:T(8,128)} async-done(((f32[1024,256]{1,0:T(8,128)}), f32[1024,256]{1,0:T(8,128)}) %all-reduce.3.cloned.1.call-update) | async-done | bytes 1048592 | tf_op jit(solution)/shard_map/psum | solution.py:68
  357.9 5.8 all_gather.14
  363.8 5.7 all_gather.15
  371.3 183.4 %while.29 = (s32[]{:T(128)}, f32[384,256]{1,0:T(8,128)}, f32[384,256]{1,0:T(8,128)S(1)}, f32[1024,256]{1,0:T(8,128)}, s32[]{:T(128)}, /*index=5*/s32[8,256]{1,0:...) while((s32[]{:T(128)}, f32[384,256]{1,0:T(8,128)}, ...), condition=%wide.region_18.19_spmd, body=%wide.region_12.18_spmd.sunk | while | flops 203302656 | bytes 9221379 | solution.py:64
  376.4 2.0 gather_fusion.7
  380.8 3.6 scatter_custom_fusion.38
  384.6 2.2 scatter_custom_fusion.39
  386.8 3.5 scatter_fusion.1
  390.3 4.0 scatter_custom_fusion.41
  399.3 2.0 gather_fusion.7
  403.6 3.6 scatter_custom_fusion.38
  407.4 2.2 scatter_custom_fusion.39
  409.7 3.5 scatter_fusion.1
  413.2 4.0 scatter_custom_fusion.41
  422.1 2.0 gather_fusion.7
  426.4 3.6 scatter_custom_fusion.38
  430.2 2.2 scatter_custom_fusion.39
  432.5 3.5 scatter_fusion.1
  436.0 4.0 scatter_custom_fusion.41
  444.9 2.0 gather_fusion.7
  449.2 3.6 scatter_custom_fusion.38
  453.1 2.2 scatter_custom_fusion.39
  455.3 3.5 scatter_fusion.1
  458.8 4.0 scatter_custom_fusion.41
  467.7 2.0 gather_fusion.7
  472.1 3.6 scatter_custom_fusion.38
  475.9 2.2 scatter_custom_fusion.39
  478.1 3.5 scatter_fusion.1
  481.6 4.0 scatter_custom_fusion.41
  490.5 2.0 gather_fusion.7
  494.9 3.6 scatter_custom_fusion.38
  498.7 2.2 scatter_custom_fusion.39
  500.9 3.5 scatter_fusion.1
  504.4 4.0 scatter_custom_fusion.41
  513.4 2.0 gather_fusion.7
  517.7 3.6 scatter_custom_fusion.38
  521.5 2.2 scatter_custom_fusion.39
  523.8 3.5 scatter_fusion.1
  527.3 4.0 scatter_custom_fusion.41
  536.2 2.0 gather_fusion.7
  540.5 3.6 scatter_custom_fusion.38
  544.4 2.2 scatter_custom_fusion.39
  546.6 3.5 scatter_fusion.1
  550.1 4.0 scatter_custom_fusion.41
  556.8 127.4 %all-reduce.5.cloned.1.call-done = f32[1024,256]{1,0:T(8,128)} async-done(((f32[1024,256]{1,0:T(8,128)}), f32[1024,256]{1,0:T(8,128)}) %all-reduce.5.cloned.1.call-update) | async-done | bytes 1048592 | tf_op jit(solution)/shard_map/psum | solution.py:68
  684.2 2.3 multiply_subtract_fusion
  (248 shorter events, 94.2 us)
Async XLA Ops:
  8.0 346.5 %all-reduce.3.cloned.1.call-start = ((), (), s32[]{:S(2)}) async-start(), calls=%async_computation.5 | async-start | bytes 2097152 | tf_op jit(solution)/shard_map/psum | solution.py:68
  8.0 0.7 copy-start.9
  9.4 1.4 copy-start.8
  9.4 3.4 copy-start.7
  10.1 2.6 copy-start.4
  12.7 6.6 copy-start.3
  19.3 8.6 %copy-start.2 = (f32[1024,256]{1,0:T(8,128)S(1)}, f32[1024,256]{1,0:T(8,128)}, u32[]{:S(2)}) copy-start(f32[1024,256]{1,0:T(8,128)} %param.14) | copy-start | bytes 3145732
  101.0 0.7 copy-start.1
  101.7 254.2 %reduce-scatter.7.cloned.1.call-start = ((), (), s32[]{:S(2)}) async-start(), calls=%async_computation.6 | async-start | bytes 589824 | tf_op jit(solution)/shard_map/reduce_scatter | solution.py:109
  102.3 254.7 %reduce-scatter.5.cloned.1.call-start = ((), (), s32[]{:S(2)}) async-start(), calls=%async_computation.4 | async-start | bytes 589824 | tf_op jit(solution)/shard_map/reduce_scatter | solution.py:108
  102.9 581.3 %all-reduce.5.cloned.1.call-start = ((), (), s32[]{:S(2)}) async-start(), calls=%async_computation.9 | async-start | bytes 2097152 | tf_op jit(solution)/shard_map/psum | solution.py:68
  356.9 6.9 collective-permute-start
  363.8 5.7 copy-start.5
  554.7 0.7 copy-start
  555.5 131.1 %reduce-scatter.9.cloned.1.call-start = ((), (), s32[]{:S(2)}) async-start(), calls=%async_computation.7 | async-start | bytes 589824 | tf_op jit(solution)/shard_map/reduce_scatter | solution.py:108
  556.0 132.1 %reduce-scatter.11.cloned.1.call-start = ((), (), s32[]{:S(2)}) async-start(), calls=%async_computation.8 | async-start | bytes 589824 | tf_op jit(solution)/shard_map/reduce_scatter | solution.py:109
  686.5 1.6 copy-start.6
Sparse Core Ops, SparseCore 0:
  101.1 253.3 all-reduce.2
  554.9 129.2 all-reduce.4
Sparse Core Ops, SparseCore 1:
  104.4 134.6 reduce-scatter.6
  241.2 13.3 reduce-scatter.4
  558.2 10.5 reduce-scatter.8
  571.0 13.3 reduce-scatter.10
where the time goes:
time: 700 us; the launch traced here: 697 us
  waiting for transfers between devices  380 us (54%)
  other arithmetic  178 us (25%)
  local copies, waits for them, and re-layouts  74 us (11%)
  blocking collectives  23.5 us (3%)
  loops' own time  16.6 us (2%)
  between operations  15.8 us (2%)
  matrix products  9.18 us (1%)
    psum x2, waiting for transfers between devices, relation_sum(): return lax.psum(g_theta, ('bucket', 'edge'))  378 us
    scatter-add x22, other arithmetic, step(): g_right = g_right.at[dst_c].add(g_d).at[neg_c].add(g_negrows)  62.9 us
    scatter-add x11, other arithmetic, step(): g_theta = g_theta.at[rel_c].add(g_t)  43.8 us
    scatter-add x11, other arithmetic, step(): g_left = g_left.at[src_c].add(g_s)  39.1 us
    gather x11, local copies, waits for them, and re-layouts, span_grads(): negatives = right[neg_c]  21.5 us
    another operation x2, loops' own time, train(): return lax.fori_loop(0, n_live, step, init)  16.6 us
  transfers between devices with their start and end apart: 7, of which 2 were waited for; matrix products, arithmetic and copies ran while one was open for 1% of the time, Pallas kernels for 0%

commit v1 on v0

--- a/solution.py
+++ b/solution.py
@@ -2,6 +2,7 @@
 import jax.numpy as jnp
 from jax import lax
 from jax.sharding import PartitionSpec as P
+from jax.lax import all_gather
 
 ROUNDS = 2
 learn_rate = 0.05
@@ -65,7 +66,7 @@
 
 
 def relation_sum(g_theta):
-    return lax.psum(g_theta, ("bucket", "edge"))
+    return jnp.sum(all_gather(g_theta, axis_name=("bucket", "edge")), axis=0)
 
 
 def descend(slab, grad):

time: 700 us -> 827 us (1.18)
  waiting for transfers between devices: 380 us -> 491 us
  other arithmetic: 178 us -> 192 us
    psum x2 -> x0, waiting for transfers between devices: 378 us -> none  [relation_sum(): return lax.psum(g_theta, ('bucket', 'edge'))]
    all_gather x0 -> x2, waiting for transfers between devices: none -> 327 us  [relation_sum(): return jnp.sum(all_gather(g_theta, axis_name=('bucket', 'edge')), axis=0)]
    reduce_scatter x2, waiting for transfers between devices: 0.03 us -> 139 us  [body(): lax.psum_scatter(g_right, 'edge', scatter_dimension=0, tiled=True)]
    reduce_sum x0 -> x2, other arithmetic: none -> 24.8 us  [relation_sum(): return jnp.sum(all_gather(g_theta, axis_name=('bucket', 'edge')), axis=0)]
    reduce_scatter x2, waiting for transfers between devices: 0.03 us -> 24.1 us  [body(): lax.psum_scatter(g_left, 'edge', scatter_dimension=0, tiled=True)]
  transfers between devices with their start and end apart: 7 -> 7, of which waited for: 2 -> 6; matrix products, arithmetic and copies ran while one was open for 1% -> 1% of each run, Pallas kernels for 0% -> 0%
where the time goes in v1:
time: 827 us; the launch traced here: 824 us
  waiting for transfers between devices  491 us (59%)
  other arithmetic  192 us (23%)
  local copies, waits for them, and re-layouts  76.2 us (9%)
  blocking collectives  22.7 us (3%)
  loops' own time  17.4 us (2%)
  between operations  15.4 us (2%)
  matrix products  9.15 us (1%)
    all_gather x2, waiting for transfers between devices, relation_sum(): return jnp.sum(all_gather(g_theta, axis_name=('bucket', 'edge')), axis=0)  327 us
    reduce_scatter x2, waiting for transfers between devices, body(): lax.psum_scatter(g_right, 'edge', scatter_dimension=0, tiled=True)  139 us
    scatter-add x22, other arithmetic, step(): g_right = g_right.at[dst_c].add(g_d).at[neg_c].add(g_negrows)  62.9 us
    scatter-add x11, other arithmetic, step(): g_theta = g_theta.at[rel_c].add(g_t)  43.8 us
    scatter-add x11, other arithmetic, step(): g_left = g_left.at[src_c].add(g_s)  34.7 us
    reduce_sum x2, other arithmetic, relation_sum(): return jnp.sum(all_gather(g_theta, axis_name=('bucket', 'edge')), axis=0)  24.8 us
    reduce_scatter x2, waiting for transfers between devices, body(): lax.psum_scatter(g_left, 'edge', scatter_dimension=0, tiled=True)  24.1 us
    gather x11, local copies, waits for them, and re-layouts, span_grads(): negatives = right[neg_c]  21.5 us
  transfers between devices with their start and end apart: 7, of which 6 were waited for; matrix products, arithmetic and copies ran while one was open for 1% of the time, Pallas kernels for 0%

profile of v1, /device:TPU:0, one launch (start us, length us, event | category | flops | bytes accessed | tf_op | source)
XLA Modules:
  0.0 824.5 jit_solution(8552959032936717649)
XLA Ops:
  11.7 6.7 all_gather.24
  18.4 5.5 all_gather.25
  26.3 68.6 %while.28 = (s32[]{:T(128)}, f32[384,256]{1,0:T(8,128)S(1)}, f32[384,256]{1,0:T(8,128)S(1)}, f32[1024,256]{1,0:T(8,128)}, s32[]{:T(128)}, /*index=5*/s32[8,256]{...) while((s32[]{:T(128)}, f32[384,256]{1,0:T(8,128)S(1)}, ...), condition=%wide.region_7.8_spmd, body=%wide.region_1.7_spmd.sunk | while | flops 203302656 | bytes 9221379 | solution.py:65
  31.3 2.0 gather_fusion.3
  33.3 2.2 gather_fusion.1
  36.8 2.2 scatter_custom_fusion.31
  39.3 2.2 scatter_custom_fusion.32
  41.5 3.5 scatter_fusion
  45.0 4.0 scatter_custom_fusion.34
  53.9 2.0 gather_fusion.3
  55.9 2.2 gather_fusion.1
  59.5 2.2 scatter_custom_fusion.31
  61.9 2.2 scatter_custom_fusion.32
  64.1 3.5 scatter_fusion
  67.6 4.0 scatter_custom_fusion.34
  76.5 2.0 gather_fusion.3
  78.5 2.2 gather_fusion.1
  82.1 2.2 scatter_custom_fusion.31
  84.5 2.2 scatter_custom_fusion.32
  86.7 3.5 scatter_fusion
  90.2 4.0 scatter_custom_fusion.34
  98.3 124.3 %reduce-scatter.7.cloned.1.call-done = f32[192,256]{1,0:T(8,128)} async-done(((f32[384,256]{1,0:T(8,128)}), f32[192,256]{1,0:T(8,128)}) %reduce-scatter.7.cloned.1.call-update) | async-done | bytes 196624 | tf_op jit(solution)/shard_map/reduce_scatter | solution.py:110
  223.7 14.9 %reduce-scatter.5.cloned.1.call-done = f32[192,256]{1,0:T(8,128)} async-done(((f32[384,256]{1,0:T(8,128)}), f32[192,256]{1,0:T(8,128)}) %reduce-scatter.5.cloned.1.call-update) | async-done | bytes 196624 | tf_op jit(solution)/shard_map/reduce_scatter | solution.py:109
  239.6 5.3 all_gather.26
  244.9 5.3 all_gather.29
  250.1 159.1 %all-gather.5.cloned.1.call-done = f32[32768,256]{1,0:T(8,128)} async-done(((f32[1024,256]{1,0:T(8,128)}), f32[32768,256]{1,0:T(8,128)}) %all-gather.5.cloned.1.call-update) | async-done | bytes 33554448 | tf_op jit(solution)/shard_map/all_gather | solution.py:69
  409.2 12.9 %reduce_sum.56 = f32[1024,256]{1,0:T(8,128)} reduce(f32[32,1024,256]{2,1,0:T(8,128)} %bitcast.102, f32[]{:T(128)} %constant.78.clone.1), dimensions={0}, to_apply=%region_11.12 | reduce | flops 8126464 | bytes 34603012 | tf_op jit(solution)/shard_map/reduce_sum | solution.py:69
  425.3 182.9 %while.29 = (s32[]{:T(128)}, f32[384,256]{1,0:T(8,128)}, f32[384,256]{1,0:T(8,128)S(1)}, f32[1024,256]{1,0:T(8,128)}, s32[]{:T(128)}, /*index=5*/s32[8,256]{1,0:...) while((s32[]{:T(128)}, f32[384,256]{1,0:T(8,128)}, ...), condition=%wide.region_18.19_spmd, body=%wide.region_12.18_spmd.sunk | while | flops 203302656 | bytes 9221379 | solution.py:65
  434.7 3.5 scatter_custom_fusion.38
  438.5 2.2 scatter_custom_fusion.39
  440.8 3.5 scatter_fusion.1
  444.3 4.0 scatter_custom_fusion.41
  457.5 3.5 scatter_custom_fusion.38
  461.3 2.2 scatter_custom_fusion.39
  463.5 3.5 scatter_fusion.1
  467.0 4.0 scatter_custom_fusion.41
  480.3 3.5 scatter_custom_fusion.38
  484.1 2.2 scatter_custom_fusion.39
  486.3 3.5 scatter_fusion.1
  489.8 4.0 scatter_custom_fusion.41
  503.0 3.5 scatter_custom_fusion.38
  506.8 2.2 scatter_custom_fusion.39
  509.1 3.5 scatter_fusion.1
  512.6 4.0 scatter_custom_fusion.41
  525.8 3.5 scatter_custom_fusion.38
  529.6 2.2 scatter_custom_fusion.39
  531.8 3.5 scatter_fusion.1
  535.3 4.0 scatter_custom_fusion.41
  548.5 3.5 scatter_custom_fusion.38
  552.3 2.2 scatter_custom_fusion.39
  554.6 3.5 scatter_fusion.1
  558.1 4.0 scatter_custom_fusion.41
  571.3 3.5 scatter_custom_fusion.38
  575.1 2.2 scatter_custom_fusion.39
  577.3 3.5 scatter_fusion.1
  580.8 4.0 scatter_custom_fusion.41
  594.1 3.5 scatter_custom_fusion.38
  597.9 2.2 scatter_custom_fusion.39
  600.1 3.5 scatter_fusion.1
  603.6 4.0 scatter_custom_fusion.41
  609.6 9.2 %reduce-scatter.9.cloned.1.call-done = f32[192,256]{1,0:T(8,128)} async-done(((f32[384,256]{1,0:T(8,128)}), f32[192,256]{1,0:T(8,128)}) %reduce-scatter.9.cloned.1.call-update) | async-done | bytes 196624 | tf_op jit(solution)/shard_map/reduce_scatter | solution.py:109
  620.4 14.3 %reduce-scatter.11.cloned.1.call-done = f32[192,256]{1,0:T(8,128)} async-done(((f32[384,256]{1,0:T(8,128)}), f32[192,256]{1,0:T(8,128)}) %reduce-scatter.11.cloned.1.call-update) | async-done | bytes 196624 | tf_op jit(solution)/shard_map/reduce_scatter | solution.py:110
  636.4 167.9 %all-gather.7.cloned.1.call-done = f32[32768,256]{1,0:T(8,128)} async-done(((f32[1024,256]{1,0:T(8,128)}), f32[32768,256]{1,0:T(8,128)}) %all-gather.7.cloned.1.call-update) | async-done | bytes 33554448 | tf_op jit(solution)/shard_map/all_gather | solution.py:69
  804.3 11.9 %reduce_sum.57 = f32[1024,256]{1,0:T(8,128)S(1)} reduce(f32[32,1024,256]{2,1,0:T(8,128)} %bitcast.103, f32[]{:T(128)} %constant.78.clone.1), dimensions={0}, to_apply=%region_21.22 | reduce | flops 8126464 | bytes 34603012 | tf_op jit(solution)/shard_map/reduce_sum | solution.py:69
  (244 shorter events, 100.5 us)
Async XLA Ops:
  8.0 214.7 %reduce-scatter.7.cloned.1.call-start = ((), (), s32[]{:S(2)}) async-start(), calls=%async_computation.5 | async-start | bytes 589824 | tf_op jit(solution)/shard_map/reduce_scatter | solution.py:110
  26.3 196.3 %copy-start.4 = (bf16[192,256]{1,0:T(8,128)(2,1)S(1)}, bf16[192,256]{1,0:T(8,128)(2,1)}, u32[]{:S(2)}) copy-start(bf16[192,256]{1,0:T(8,128)(2,1)} %param.13) | copy-start | bytes 294916
  26.3 212.3 %copy-start.5 = (bf16[192,256]{1,0:T(8,128)(2,1)S(1)}, bf16[192,256]{1,0:T(8,128)(2,1)}, u32[]{:S(2)}) copy-start(bf16[192,256]{1,0:T(8,128)(2,1)} %param.12) | copy-start | bytes 294916
  94.9 0.7 copy-start
  94.9 0.9 copy-start.3
  94.9 327.2 %copy-start.2 = (f32[1024,256]{1,0:T(8,128)S(1)}, f32[1024,256]{1,0:T(8,128)}, u32[]{:S(2)}) copy-start(f32[1024,256]{1,0:T(8,128)} %get-tuple-element.544) | copy-start | bytes 3145732
  95.7 142.9 %reduce-scatter.5.cloned.1.call-start = ((), (), s32[]{:S(2)}) async-start(), calls=%async_computation.4 | async-start | bytes 589824 | tf_op jit(solution)/shard_map/reduce_scatter | solution.py:109
  96.4 312.8 %all-gather.5.cloned.1.call-start = ((), (), s32[]{:S(2)}) async-start(), calls=%async_computation.8 | async-start | bytes 34603008 | tf_op jit(solution)/shard_map/all_gather | solution.py:69
  97.0 521.8 %reduce-scatter.9.cloned.1.call-start = ((), (), s32[]{:S(2)}) async-start(), calls=%async_computation.6 | async-start | bytes 589824 | tf_op jit(solution)/shard_map/reduce_scatter | solution.py:109
  223.7 21.2 %collective-permute-start = (bf16[192,256]{1,0:T(8,128)(2,1)S(1)}, bf16[192,256]{1,0:T(8,128)(2,1)S(1)}, u32[]{:S(2)}, u32[]{:S(2)}) collective-permute-start(bf16[192,256]{1,0:T(8,128)(2,1)S(1)} %subtract_convert_fusion.2), channel_id=1, source_target_pairs={{30,0},{0,2},{2,4},{4,6},{6,8},{8,10},{10,12},{12,14},{14,16},{16,... | collective-permute-start | bytes 294920 | tf_op jit(solution)/shard_map/ppermute | solution.py:15
  244.9 180.5 %copy-start.6 = (bf16[192,256]{1,0:T(8,128)(2,1)}, bf16[192,256]{1,0:T(8,128)(2,1)S(1)}, u32[]{:S(2)}) copy-start(bf16[192,256]{1,0:T(8,128)(2,1)S(1)} %collective-permute-done) | copy-start | bytes 294916
  608.2 0.8 copy-start.1
  608.3 26.5 %reduce-scatter.11.cloned.1.call-start = ((), (), s32[]{:S(2)}) async-start(), calls=%async_computation.7 | async-start | bytes 589824 | tf_op jit(solution)/shard_map/reduce_scatter | solution.py:110
  609.0 195.3 %all-gather.7.cloned.1.call-start = ((), (), s32[]{:S(2)}) async-start(), calls=%async_computation.9 | async-start | bytes 34603008 | tf_op jit(solution)/shard_map/all_gather | solution.py:69
Sparse Core Ops, SparseCore 0:
  95.8 126.8 reduce-scatter.6
  224.9 13.6 reduce-scatter.4
  608.4 10.3 reduce-scatter.8
  620.9 13.7 reduce-scatter.10
Sparse Core Ops, SparseCore 1:
  100.6 308.6 all-gather.4
  613.2 191.1 all-gather.6
